TPU v7x, 256 devices: a whole 4x4x8 slice. The times are simulated.
256 devices in a mesh: section: 4 (over z_hi), dp: 16 (over x, z_lo, core), feat: 4 (over y).
Axes of the slice: x: 4, y: 4, z: 8 (z_hi: 4, z_lo: 2; z = z_hi * 2 + z_lo), core: 2. Of those that a mesh axis runs over, the one named last changes fastest.
Arguments:
- tokens: bfloat16 [4096, 16384], P('dp', 'feat'), may hold values from -6 to 6
- basis: bfloat16 [2048, 16384], P('section', 'feat'), may hold values from -0.046875 to 0.046875
Outputs:
- basis_step: bfloat16 [2048, 16384], P('section', 'feat')
- projections: float32 [4096, 2048], P('dp', 'section')
All inputs are finite; a program needn't handle non-finite values.
Results may differ from a plain program's by a relative error of at most 0.034.
Values may be sent and summed in bfloat16 or wider, within the bound.
A program may use at most 64 MiB of HBM per device.

v0:
```python
import math
import jax
import jax.numpy as jnp
from jax import lax
from jax.sharding import PartitionSpec as P

D = 16384
BF16 = jnp.bfloat16
F32 = jnp.float32


def dot(a, b, ca, cb):
    return lax.dot_general(a, b, (((ca,), (cb,)), ((), ())), preferred_element_type=F32)


def shards(tokens, basis):
    s = lax.axis_index("section")
    d = lax.axis_index("dp")
    n_sec = lax.axis_size("section")
    n_dp = lax.axis_size("dp")
    rows, width = tokens.shape
    block = basis.shape[0]
    piece = block // n_dp
    scaling = math.sqrt(D) / (rows * n_dp)
    mine = lax.dynamic_slice_in_dim(basis, d * piece, piece, 0)
    slices = lax.all_gather(mine, "section").reshape(n_sec * piece, width)
    cross = dot(slices, basis, 1, 1).astype(BF16)
    cross = lax.psum(cross, "feat")
    cross = lax.all_gather(cross, ("section", "dp"))
    cross = cross.reshape(n_sec, n_dp, n_sec, piece, block)
    cross = cross.transpose(0, 2, 1, 3, 4).reshape(n_sec, n_sec, block, block)
    scores = dot(tokens, basis, 1, 1).astype(BF16)
    scores = lax.psum_scatter(scores, "feat", scatter_dimension=0, tiled=True)
    scores = lax.all_gather(scores, "section")
    rounded = []
    for b in range(n_sec):
        y = scores[b].astype(F32)
        for j in range(b):
            y = y - dot(rounded[j], cross[b, j], 1, 0)
        rounded.append(y.astype(BF16))
    q = jnp.stack(rounded)
    q = lax.all_gather(q, "feat", axis=1, tiled=True)
    q_mine = lax.dynamic_index_in_dim(q, s, 0, keepdims=False)
    projections = q_mine.astype(F32)
    gram = jnp.einsum("jrc,rk->jck", q, q_mine, preferred_element_type=F32)
    gram = gram.astype(BF16).reshape(n_sec, n_dp, piece, block).transpose(1, 0, 2, 3)
    gram = lax.psum_scatter(gram, "dp", scatter_dimension=0, tiled=True)[0]
    col = d * piece + lax.broadcasted_iota(jnp.int32, (n_sec, piece, block), 1)
    row = lax.broadcasted_iota(jnp.int32, (n_sec, piece, block), 2)
    j = lax.broadcasted_iota(jnp.int32, (n_sec, piece, block), 0)
    keep = (j < s) | (j == s) & (col <= row)
    gram = jnp.where(keep, gram, jnp.zeros_like(gram)).reshape(n_sec * piece, block)
    part = dot(q_mine, tokens, 0, 0) - dot(gram, slices, 0, 0)
    total = lax.psum(part.astype(BF16), "dp")
    basis_step = (total.astype(F32) * scaling).astype(BF16)
    return (basis_step, projections)


def solution(mesh):
    in_specs = (P("dp", "feat"), P("section", "feat"))
    out_specs = (P("section", "feat"), P("dp", "section"))
    return jax.shard_map(shards, mesh=mesh, in_specs=in_specs, out_specs=out_specs, check_vma=False)
```

profile of v0, /device:TPU:8, one launch (start us, length us, event | category | flops | bytes accessed | tf_op | source)
XLA Modules:
  0.0 516.0 jit_solution(6253353343966309557)
XLA Ops:
  7.2 1.8 constant_dynamic-slice_fusion
  9.1 39.6 %all-gather.10.cloned.1.call-done = bf16[128,4096]{1,0:T(8,128)(2,1)} async-done(((bf16[32,4096]{1,0:T(8,128)(2,1)}), bf16[128,4096]{1,0:T(8,128)(2,1)}) %all-gather.10.cloned.1.call-update) | async-done | bytes 1048592 | tf_op jit(solution)/shard_map/all_gather | solution.py:26
  48.7 4.7 fusion.1
  53.5 4.2 convolution_convert_fusion.1
  57.7 38.6 %all-reduce.3.cloned.1.call-done = bf16[1,128,512]{2,1,0:T(8,128)(2,1)} async-done(((bf16[1,128,512]{2,1,0:T(8,128)(2,1)}), bf16[1,128,512]{2,1,0:T(8,128)(2,1)}) %all-reduce.3.cloned.1.call-update) | async-done | bytes 131088 | tf_op jit(solution)/shard_map/psum | solution.py:28
  96.4 26.1 %reduce-scatter.3.cloned.1.call-done = bf16[64,512]{1,0:T(8,128)(2,1)} async-done(((bf16[256,512]{1,0:T(8,128)(2,1)}), bf16[64,512]{1,0:T(8,128)(2,1)}) %reduce-scatter.3.cloned.1.call-update) | async-done | bytes 65552 | tf_op jit(solution)/shard_map/reduce_scatter | solution.py:33
  122.5 17.4 %all-gather = bf16[256,512]{1,0:T(8,128)(2,1)S(1)} all-gather(bf16[64,512]{1,0:T(8,128)(2,1)} %reduce-scatter.3.cloned.1.call-done), channel_id=2, replica_groups=mesh['section'=4,'dp'=16,'feat'=4] {'section'}, dimensions={0}, use_global_device_ids=true | all-gather | bytes 327680 | tf_op jit(solution)/shard_map/all_gather | solution.py:34
  139.9 106.2 %all-gather.6.cloned.1.call-done = bf16[64,128,512]{2,1,0:T(8,128)(2,1)} async-done(((bf16[1,128,512]{2,1,0:T(8,128)(2,1)}), bf16[64,128,512]{2,1,0:T(8,128)(2,1)}) %all-gather.6.cloned.1.call-update) | async-done | bytes 8388624 | tf_op jit(solution)/shard_map/all_gather | solution.py:29
  246.1 8.3 %copy.8 = bf16[4,4,16,32,512]{4,3,2,1,0:T(8,128)(2,1)} copy(bf16[4,4,16,32,512]{4,3,1,2,0:T(8,128)(2,1)} %bitcast.67) | data formatting | bytes 16777216 | tf_op jit(solution)/shard_map/transpose | solution.py:31
  254.4 1.2 fusion.2
  255.6 1.2 convolution_subtract_fusion.4
  256.9 1.2 convolution_subtract_fusion.2
  258.1 1.2 fusion.3
  259.4 1.2 convolution_subtract_fusion.1
  260.6 1.2 fusion.5
  262.7 24.5 %all-gather.8.cloned.1.call-done = bf16[4,256,512]{2,1,0:T(8,128)(2,1)} async-done(((bf16[4,64,512]{2,1,0:T(8,128)(2,1)}), bf16[4,256,512]{2,1,0:T(8,128)(2,1)}) %all-gather.8.cloned.1.call-update) | async-done | bytes 1048592 | tf_op jit(solution)/shard_map/all_gather | solution.py:42
  287.2 2.0 convolution_convert_fusion
  289.2 1.6 copy.11
  290.8 68.4 %reduce-scatter.5.cloned.1.call-done = bf16[1,4,32,512]{3,2,1,0:T(8,128)(2,1)} async-done(((bf16[16,4,32,512]{3,2,1,0:T(8,128)(2,1)}), bf16[1,4,32,512]{3,2,1,0:T(8,128)(2,1)}) %reduce-scatter.5.cloned.1.call-update) | async-done | bytes 131088 | tf_op jit(solution)/shard_map/reduce_scatter | solution.py:47
  359.3 2.7 fusion.13
  362.0 3.4 fusion
  365.5 0.9 bitcast_convert_fusion
  366.3 137.6 %all-reduce.5.cloned.1.call-done = bf16[512,4096]{1,0:T(8,128)(2,1)} async-done(((bf16[512,4096]{1,0:T(8,128)(2,1)}), bf16[512,4096]{1,0:T(8,128)(2,1)}) %all-reduce.5.cloned.1.call-update) | async-done | bytes 4194320 | tf_op jit(solution)/shard_map/psum | solution.py:54
  503.9 5.2 %multiply_convert_fusion = bf16[512,4096]{1,0:T(8,128)(2,1)} fusion(bf16[512,4096]{1,0:T(8,128)(2,1)} %all-reduce.5.cloned.1.call-done), kind=kLoop, calls=%fused_computation.2 | loop fusion | flops 6291456 | bytes 8388608 | tf_op jit(solution)/shard_map/convert_element_type | solution.py:55
  (22 shorter events, 1.2 us)
Async XLA Ops:
  7.2 46.3 %copy-start = (bf16[256,4096]{1,0:T(8,128)(2,1)S(1)}, bf16[256,4096]{1,0:T(8,128)(2,1)}, u32[]{:S(2)}) copy-start(bf16[256,4096]{1,0:T(8,128)(2,1)} %param.2) | copy-start | bytes 6291460
  7.2 41.5 %all-gather.10.cloned.1.call-start = ((), (), s32[]{:S(2)}) async-start(), calls=%async_computation.8 | async-start | bytes 1310720 | tf_op jit(solution)/shard_map/all_gather | solution.py:26
  9.1 87.2 %all-reduce.3.cloned.1.call-start = ((), (), s32[]{:S(2)}) async-start(), calls=%async_computation.3 | async-start | bytes 262144 | tf_op jit(solution)/shard_map/psum | solution.py:28
  53.4 69.1 %reduce-scatter.3.cloned.1.call-start = ((), (), s32[]{:S(2)}) async-start(), calls=%async_computation.2 | async-start | bytes 327680 | tf_op jit(solution)/shard_map/reduce_scatter | solution.py:33
  57.7 188.4 %all-gather.6.cloned.1.call-start = ((), (), s32[]{:S(2)}) async-start(), calls=%async_computation.4 | async-start | bytes 8519680 | tf_op jit(solution)/shard_map/all_gather | solution.py:29
  96.3 190.8 %all-gather.8.cloned.1.call-start = ((), (), s32[]{:S(2)}) async-start(), calls=%async_computation.5 | async-start | bytes 1310720 | tf_op jit(solution)/shard_map/all_gather | solution.py:42
  262.7 96.6 %reduce-scatter.5.cloned.1.call-start = ((), (), s32[]{:S(2)}) async-start(), calls=%async_computation.6 | async-start | bytes 2228224 | tf_op jit(solution)/shard_map/reduce_scatter | solution.py:47
  290.8 213.1 %all-reduce.5.cloned.1.call-start = ((), (), s32[]{:S(2)}) async-start(), calls=%async_computation.7 | async-start | bytes 8388608 | tf_op jit(solution)/shard_map/psum | solution.py:54
  359.3 2.7 copy-start.1
Sparse Core Ops, SparseCore 0:
  10.4 38.2 all-gather.9
  53.5 42.7 all-reduce.2
  99.6 22.8 reduce-scatter.2
  124.2 121.8 all-gather.5
  262.8 24.3 all-gather.7
  290.9 68.3 reduce-scatter.4
  365.6 138.2 all-reduce.4
where the time goes:
time: 517 us; the launch traced here: 516 us
  waiting for transfers between devices  441 us (85%)
  matrix products  24.5 us (5%)
  blocking collectives  17.4 us (3%)
  between operations  14.2 us (3%)
  local copies, waits for them, and re-layouts  11.7 us (2%)
  other arithmetic  6.85 us (1%)
    psum x1, waiting for transfers between devices, shards(): total = lax.psum(part.astype(BF16), 'dp')  138 us
    all_gather x1, waiting for transfers between devices, shards(): cross = lax.all_gather(cross, ('section', 'dp'))  106 us
    reduce_scatter x1, waiting for transfers between devices, shards(): gram = lax.psum_scatter(gram, 'dp', scatter_dimension=0, tiled=True)[0]  68.4 us
    all_gather x1, waiting for transfers between devices, shards(): slices = lax.all_gather(mine, 'section').reshape(n_sec * piece, width)  39.6 us
    psum x1, waiting for transfers between devices, shards(): cross = lax.psum(cross, 'feat')  38.6 us
    reduce_scatter x1, waiting for transfers between devices, shards(): scores = lax.psum_scatter(scores, 'feat', scatter_dimension=0, tiled=True)  26.1 us
    all_gather x1, waiting for transfers between devices, shards(): q = lax.all_gather(q, 'feat', axis=1, tiled=True)  24.5 us
    dot_general x10, matrix products, dot(): lax.dot_general(a, b, (((ca,), (cb,)), ((), ())), preferred_element_type=...  22.5 us
  transfers between devices with their start and end apart: 7, of which 7 were waited for; matrix products, arithmetic and copies ran while one was open for 1% of the time, Pallas kernels for 0%

commit v1 on v0

--- a/solution.py
+++ b/solution.py
@@ -25,7 +25,9 @@
     mine = lax.dynamic_slice_in_dim(basis, d * piece, piece, 0)
     slices = lax.all_gather(mine, "section").reshape(n_sec * piece, width)
     cross = dot(slices, basis, 1, 1).astype(BF16)
-    cross = lax.psum(cross, "feat")
+    cross = cross
+    for hop in (1, 2):
+        cross = cross + lax.ppermute(cross, "feat", [(dev, dev ^ hop) for dev in range(4)])
     cross = lax.all_gather(cross, ("section", "dp"))
     cross = cross.reshape(n_sec, n_dp, n_sec, piece, block)
     cross = cross.transpose(0, 2, 1, 3, 4).reshape(n_sec, n_sec, block, block)

time: 517 us -> 455 us (0.88)
  waiting for transfers between devices: 441 us -> 377 us
    psum x1 -> x0, waiting for transfers between devices: 38.6 us -> none  [shards(): cross = lax.psum(cross, 'feat')]
    reduce_scatter x1, waiting for transfers between devices: 26.1 us -> 0.02 us  [shards(): scores = lax.psum_scatter(scores, 'feat', scatter_dimension=0, tiled=True)]
    ppermute x0 -> x2, waiting for transfers between devices: none -> 8.89 us  [shards(): lax.ppermute(cross, 'feat', [(dev, dev ^ hop) for dev in range(4)])]
    reshape x0 -> x1, local copies, waits for them, and re-layouts: none -> 8.28 us  [shards(): cross = cross.reshape(n_sec, n_dp, n_sec, piece, block)]
    transpose x1 -> x0, local copies, waits for them, and re-layouts: 8.28 us -> none  [shards(): cross = cross.transpose(0, 2, 1, 3, 4).reshape(n_sec, n_sec, block, block)]
  transfers between devices with their start and end apart: 7 -> 8, of which waited for: 7 -> 7; matrix products, arithmetic and copies ran while one was open for 1% -> 2% of each run, Pallas kernels for 0% -> 0%
where the time goes in v1:
time: 455 us
  waiting for transfers between devices  377 us (83%)
  matrix products  23.8 us (5%)
  between operations  15.8 us (3%)
  blocking collectives  15.4 us (3%)
  local copies, waits for them, and re-layouts  11.7 us (3%)
  other arithmetic  7.57 us (2%)
    psum x1, waiting for transfers between devices, shards(): total = lax.psum(part.astype(BF16), 'dp')  137 us
    all_gather x1, waiting for transfers between devices, shards(): cross = lax.all_gather(cross, ('section', 'dp'))  103 us
    reduce_scatter x1, waiting for transfers between devices, shards(): gram = lax.psum_scatter(gram, 'dp', scatter_dimension=0, tiled=True)[0]  68.5 us
    all_gather x1, waiting for transfers between devices, shards(): slices = lax.all_gather(mine, 'section').reshape(n_sec * piece, width)  35.4 us
    all_gather x1, waiting for transfers between devices, shards(): q = lax.all_gather(q, 'feat', axis=1, tiled=True)  24.4 us
    dot_general x10, matrix products, dot(): lax.dot_general(a, b, (((ca,), (cb,)), ((), ())), preferred_element_type=...  21.8 us
    all_gather x1, blocking collectives, shards(): scores = lax.all_gather(scores, 'section')  15.4 us
  transfers between devices with their start and end apart: 8, of which 7 were waited for; matrix products, arithmetic and copies ran while one was open for 2% of the time, Pallas kernels for 0%

profile of v1, /device:TPU:8, one launch (start us, length us, event | category | flops | bytes accessed | tf_op | source)
XLA Modules:
  0.0 454.8 jit_solution(6554688220059178678)
XLA Ops:
  8.1 1.8 constant_dynamic-slice_fusion
  10.0 4.2 convolution_convert_fusion.1
  14.2 35.4 %all-gather.9.cloned.1.call-done = bf16[128,4096]{1,0:T(8,128)(2,1)} async-done(((bf16[32,4096]{1,0:T(8,128)(2,1)}), bf16[128,4096]{1,0:T(8,128)(2,1)}) %all-gather.9.cloned.1.call-update) | async-done | bytes 1048592 | tf_op jit(solution)/shard_map/all_gather | solution.py:26
  49.7 4.0 convolution_convert_fusion.2
  54.3 4.5 collective-permute-done
  58.9 2.2 collective-permute-start.1
  61.1 4.3 collective-permute-done.1
  66.3 15.4 %all-gather = bf16[256,512]{1,0:T(8,128)(2,1)S(1)} all-gather(bf16[64,512]{1,0:T(8,128)(2,1)} %reduce-scatter.3.cloned.1.call-done), channel_id=2, replica_groups=mesh['section'=4,'dp'=16,'feat'=4] {'section'}, dimensions={0}, use_global_device_ids=true | all-gather | bytes 327680 | tf_op jit(solution)/shard_map/all_gather | solution.py:36
  81.7 102.9 %all-gather.11.cloned.1.call-done = bf16[8192,512]{1,0:T(8,128)(2,1)} async-done(((bf16[128,512]{1,0:T(8,128)(2,1)}), bf16[8192,512]{1,0:T(8,128)(2,1)}) %all-gather.11.cloned.1.call-update) | async-done | bytes 8388624 | tf_op jit(solution)/shard_map/all_gather | solution.py:31
  184.5 8.3 %copy.5 = bf16[4,16,4,32,512]{4,3,1,2,0:T(8,128)(2,1)} copy(bf16[4,16,4,32,512]{4,3,2,1,0:T(8,128)(2,1)} %bitcast.65) | data formatting | bytes 16777216 | tf_op jit(solution)/shard_map/reshape | solution.py:32
  192.8 1.2 fusion.1
  194.1 1.2 convolution_subtract_fusion.4
  195.3 1.2 convolution_subtract_fusion.2
  196.6 1.2 fusion.2
  197.8 1.2 convolution_subtract_fusion.1
  199.1 1.2 fusion.4
  201.2 24.4 %all-gather.7.cloned.1.call-done = bf16[4,256,512]{2,1,0:T(8,128)(2,1)} async-done(((bf16[4,64,512]{2,1,0:T(8,128)(2,1)}), bf16[4,256,512]{2,1,0:T(8,128)(2,1)}) %all-gather.7.cloned.1.call-update) | async-done | bytes 1048592 | tf_op jit(solution)/shard_map/all_gather | solution.py:44
  225.6 2.0 convolution_convert_fusion
  227.6 1.6 copy.8
  229.3 68.5 %reduce-scatter.5.cloned.1.call-done = bf16[1,4,32,512]{3,2,1,0:T(8,128)(2,1)} async-done(((bf16[16,4,32,512]{3,2,1,0:T(8,128)(2,1)}), bf16[1,4,32,512]{3,2,1,0:T(8,128)(2,1)}) %reduce-scatter.5.cloned.1.call-update) | async-done | bytes 131088 | tf_op jit(solution)/shard_map/reduce_scatter | solution.py:49
  297.8 2.7 fusion.12
  300.5 3.4 fusion
  304.8 137.1 %all-reduce.2.cloned.1.call-done = bf16[512,4096]{1,0:T(8,128)(2,1)} async-done(((bf16[512,4096]{1,0:T(8,128)(2,1)}), bf16[512,4096]{1,0:T(8,128)(2,1)}) %all-reduce.2.cloned.1.call-update) | async-done | bytes 4194320 | tf_op jit(solution)/shard_map/psum | solution.py:56
  441.9 5.2 %multiply_convert_fusion = bf16[512,4096]{1,0:T(8,128)(2,1)} fusion(bf16[512,4096]{1,0:T(8,128)(2,1)} %all-reduce.2.cloned.1.call-done), kind=kLoop, calls=%fused_computation.2 | loop fusion | flops 6291456 | bytes 8388608 | tf_op jit(solution)/shard_map/convert_element_type | solution.py:57
  (25 shorter events, 3.4 us)
Async XLA Ops:
  8.0 2.0 copy-start
  8.0 41.6 %all-gather.9.cloned.1.call-start = ((), (), s32[]{:S(2)}) async-start(), calls=%async_computation.6 | async-start | bytes 1310720 | tf_op jit(solution)/shard_map/all_gather | solution.py:26
  9.9 56.4 %reduce-scatter.3.cloned.1.call-start = ((), (), s32[]{:S(2)}) async-start(), calls=%async_computation.2 | async-start | bytes 327680 | tf_op jit(solution)/shard_map/reduce_scatter | solution.py:35
  14.2 170.4 %all-gather.11.cloned.1.call-start = ((), (), s32[]{:S(2)}) async-start(), calls=%async_computation.7 | async-start | bytes 8519680 | tf_op jit(solution)/shard_map/all_gather | solution.py:31
  53.7 5.2 %collective-permute-start = (bf16[128,512]{1,0:T(8,128)(2,1)S(1)}, bf16[128,512]{1,0:T(8,128)(2,1)S(1)}, u32[]{:S(2)}, u32[]{:S(2)}) collective-permute-start(bf16[128,512]{1,0:T(8,128)(2,1)S(1)} %convolution_convert_fusion.2), channel_id=1, source_target_pairs={{0,1},{1,0},{2,3},{3,2},{4,5},{5,4},{6,7},{7,6},{8,9},{9,8},{10,11... | collective-permute-start | bytes 393224 | tf_op jit(solution)/shard_map/ppermute | solution.py:30
  58.9 6.6 %collective-permute-start.1 = (bf16[128,512]{1,0:T(8,128)(2,1)S(1)}, bf16[128,512]{1,0:T(8,128)(2,1)S(1)}, u32[]{:S(2)}, u32[]{:S(2)}) collective-permute-start(bf16[128,512]{1,0:T(8,128)(2,1)S(1)} %add.27), channel_id=1, source_target_pairs={{0,2},{1,3},{2,0},{3,1},{4,6},{5,7},{6,4},{7,5},{8,10},{9,11},{10,... | collective-permute-start | bytes 393224 | tf_op jit(solution)/shard_map/ppermute | solution.py:30
  66.2 159.4 %all-gather.7.cloned.1.call-start = ((), (), s32[]{:S(2)}) async-start(), calls=%async_computation.3 | async-start | bytes 1310720 | tf_op jit(solution)/shard_map/all_gather | solution.py:44
  201.1 96.7 %reduce-scatter.5.cloned.1.call-start = ((), (), s32[]{:S(2)}) async-start(), calls=%async_computation.4 | async-start | bytes 2228224 | tf_op jit(solution)/shard_map/reduce_scatter | solution.py:49
  229.2 212.8 %all-reduce.2.cloned.1.call-start = ((), (), s32[]{:S(2)}) async-start(), calls=%async_computation.5 | async-start | bytes 8388608 | tf_op jit(solution)/shard_map/psum | solution.py:56
  297.8 2.7 copy-start.1
Sparse Core Ops, SparseCore 0:
  11.4 38.2 all-gather.8
  66.3 118.1 all-gather.10
Sparse Core Ops, SparseCore 1:
  14.2 24.2 reduce-scatter.2
  201.2 24.3 all-gather.6
  229.3 68.5 reduce-scatter.4
  304.0 137.8 all-reduce.1
